TPU v7x, 512 devices: a whole 4x8x8 slice. The times are simulated.
512 devices in a mesh: seq: 32 (over x, z), tp: 16 (over y, core).
Axes of the slice: x: 4, y: 8, z: 8, core: 2. Of those that a mesh axis runs over, the one named last changes fastest.
Arguments:
- residual: bfloat16 [6144, 8192], P('seq', 'tp'), may hold values from -6 to 6
- attention: bfloat16 [1536, 8192], P('seq'), may hold values from -6 to 6
- quantized_codes: int32 [8192, 8192], P('seq', 'tp'), may hold values from 0 to 15
- absmax: float32 [8192, 128], P('seq', 'tp'), may hold values from 0.005 to 0.05
- adapter_down: bfloat16 [8192, 64], P('seq'), may hold values from -0.0625 to 0.0625
- adapter_up: bfloat16 [64, 8192], P(None, 'tp'), may hold values from -0.75 to 0.75
- routed_slot_gate: float32 [1536], P('seq'), may hold values from 0.2 to 1
- selected: int32 [1536], P('seq'), may hold values from 0 to 191, as said below
- counts: int32 [32], P('seq'), may hold values from 1 to 48, 768 in all
- cotangent: bfloat16 [6144, 8192], P('seq', 'tp'), may hold values from -0.59765625 to 0.59765625
Outputs:
- outgoing_residual: bfloat16 [6144, 8192], P('seq', 'tp')
- attention_output_grad: bfloat16 [1536, 8192], P(None, 'seq')
- adapter_down_gradient: float32 [8192, 64], P('seq')
- adapter_up_gradient: float32 [64, 8192], P(None, 'tp')
- router_gate_gradient: float32 [1536], P('seq')
Inputs may be any that keep to these rules, and one draw needn't show every extreme that they name: `counts`: every shard has at least one live slot, all shards together have 768, and some shard has all 48 slots live. `selected`: within each shard's 48 slots the entries are distinct token positions of that shard; only the first counts entries of a shard are live.
All inputs are finite; a program needn't handle non-finite values.
Results may differ from a plain program's by a relative error of at most 0.0058.
Values may be sent and summed in bfloat16 or wider, within the bound.
A program may use at most 64 MiB of HBM per device.

v0:
```python
import jax
import jax.numpy as jnp
from jax import lax
from jax.sharding import PartitionSpec as P

LEVELS = (
    -1.0,
    -0.6961928009986877,
    -0.5250730514526367,
    -0.39491748809814453,
    -0.28444138169288635,
    -0.18477343022823334,
    -0.09105003625154495,
    0.0,
    0.07958029955625534,
    0.16093020141124725,
    0.24611230194568634,
    0.33791524171829224,
    0.44070982933044434,
    0.5626170039176941,
    0.7229568362236023,
    1.0,
)
adapter_scale = 0.25


def precise_matmul(left, right):
    return jnp.dot(left, right, precision=lax.Precision.HIGHEST, preferred_element_type=jnp.float32)


def dequantize(quantized_codes, absmax):
    quantile_levels = jnp.zeros(quantized_codes.shape, jnp.float32)
    for level_code in range(16):
        quantile_levels = quantile_levels + jnp.where(
            quantized_codes == level_code, LEVELS[level_code], 0.0
        )
    block_size = quantized_codes.shape[1] // absmax.shape[1]
    scales = jnp.repeat(absmax, block_size, axis=1)
    return (quantile_levels * scales).astype(jnp.bfloat16)


def body(
    residual,
    attention,
    quantized_codes,
    absmax,
    adapter_down,
    adapter_up,
    routed_slot_gate,
    selected,
    counts,
    cotangent,
):
    projection_weight = dequantize(quantized_codes, absmax)
    adapter_up_single32 = adapter_up.astype(jnp.float32)
    home_slots = attention.shape[0]
    live_slot = jnp.arange(home_slots, dtype=jnp.int32) < counts[0]
    target = jnp.where(live_slot, selected, residual.shape[0])
    full_w, full_a = (
        lax.all_gather(projection_weight, "seq", axis=0, tiled=True),
        lax.all_gather(adapter_down, "seq", axis=0, tiled=True),
    )
    adapter_product = jnp.dot(attention, full_a, preferred_element_type=jnp.float32)
    block_output = jnp.dot(
        attention, full_w, preferred_element_type=jnp.float32
    ) + adapter_scale * precise_matmul(adapter_product, adapter_up_single32)
    picked = residual[selected].astype(jnp.float32)
    updated = (picked + routed_slot_gate[:, None] * block_output).astype(jnp.bfloat16)
    outgoing_residual = residual.at[target].set(updated, mode="drop")
    upstream = jnp.where(live_slot[:, None], cotangent[selected].astype(jnp.float32), 0.0)
    gate_part = jnp.sum(upstream * block_output, axis=1)
    output_gradient = (routed_slot_gate[:, None] * upstream).astype(jnp.bfloat16)
    head_part = jnp.dot(output_gradient, full_w.T, preferred_element_type=jnp.float32)
    adapter_rank_piece = adapter_scale * jnp.dot(
        output_gradient, adapter_up.T, preferred_element_type=jnp.float32
    )
    head_full, rank_full, router_gate_gradient = lax.psum(
        (head_part, adapter_rank_piece, gate_part), "tp"
    )
    adapter_rank_gradient = rank_full.astype(jnp.bfloat16)
    home_grad = (
        head_full + jnp.dot(adapter_rank_gradient, full_a.T, preferred_element_type=jnp.float32)
    ).astype(jnp.bfloat16)
    attention_output_grad = lax.all_to_all(
        home_grad, "seq", split_axis=1, concat_axis=0, tiled=True
    )
    adapter_down_gradient = lax.psum_scatter(
        jnp.dot(attention.T, adapter_rank_gradient, preferred_element_type=jnp.float32),
        "seq",
        scatter_dimension=0,
        tiled=True,
    )
    up_factor_piece = adapter_scale * precise_matmul(
        adapter_product.T, output_gradient.astype(jnp.float32)
    )
    adapter_up_gradient = lax.psum(up_factor_piece, "seq")
    return (
        outgoing_residual,
        attention_output_grad,
        adapter_down_gradient,
        adapter_up_gradient,
        router_gate_gradient,
    )


def solution(mesh):
    return jax.shard_map(
        body,
        mesh=mesh,
        in_specs=(
            P("seq", "tp"),
            P("seq", None),
            P("seq", "tp"),
            P("seq", "tp"),
            P("seq", None),
            P(None, "tp"),
            P("seq"),
            P("seq"),
            P("seq"),
            P("seq", "tp"),
        ),
        out_specs=(P("seq", "tp"), P(None, "seq"), P("seq", None), P(None, "tp"), P("seq")),
        check_vma=False,
    )
```

profile of v0, /device:TPU:8, one launch (start us, length us, event | category | flops | bytes accessed | tf_op | source)
XLA Modules:
  0.0 714.8 jit_solution(8451295507987079360)
XLA Ops:
  7.2 0.0 copy-start
  7.2 0.0 copy-start.7
  7.2 0.0 copy-start.4
  7.2 0.0 copy-start.6
  7.2 0.0 all-gather.3.cloned.1.call-start
  7.3 1.3 copy.33
  8.6 2.2 fusion.2
  10.8 0.0 all-gather.3.cloned.1.call-update
  10.8 0.0 all-gather.5.cloned.1.call-start
  10.8 0.7 all-gather.5.cloned.1.call-update
  11.5 0.0 all-reduce.4.cloned.1.call-start
  12.2 0.0 copy-done.7
  12.3 0.0 copy-done.4
  12.3 0.7 gather_fusion
  13.0 0.0 copy-start.5
  13.0 113.0 %all-gather.3.cloned.1.call-done = bf16[8192,512]{0,1:T(8,128)(2,1)} async-done(((bf16[256,512]{0,1:T(8,128)(2,1)}), bf16[8192,512]{0,1:T(8,128)(2,1)}) %all-gather.3.cloned.1.call-update) | async-done | bytes 8388624 | tf_op jit(solution)/shard_map/all_gather | solution.py:60
  126.0 0.0 copy-done.6
  126.0 6.1 fusion.8
  132.1 0.0 all-reduce.4.cloned.1.call-update
  132.1 0.0 all-reduce.6.cloned.1.call-start
  132.2 0.0 copy-done.5
  132.2 0.2 convolution_multiply_fusion.2
  132.4 71.0 %all-gather.5.cloned.1.call-done = bf16[8192,64]{0,1:T(8,128)(2,1)} async-done(((bf16[256,64]{0,1:T(8,128)(2,1)}), bf16[8192,64]{0,1:T(8,128)(2,1)}) %all-gather.5.cloned.1.call-update) | async-done | bytes 1048592 | tf_op jit(solution)/shard_map/all_gather | solution.py:61
  203.4 0.0 copy-done
  203.4 1.6 fusion.9
  205.1 0.9 convolution_multiply_fusion
  206.0 0.0 all-reduce.6.cloned.1.call-update
  206.0 0.0 reduce-scatter.2.cloned.1.call-start
  206.1 6.0 convolution_bitcast_fusion.1
  212.1 0.3 multiply_reduce_fusion
  212.4 42.8 %all-reduce = (bf16[48,64]{1,0:T(8,128)(2,1)S(1)}, f32[48]{0:T(128)}) all-reduce(f32[48,64]{1,0:T(8,128)S(1)} %convolution_multiply_fusion.2, f32[48]{0:T(128)S(1)} %get-tuple-element.9), channel_id=1, replica_groups=mesh['seq'=32,'tp'=16] {'tp'}, use_global_device_ids=true, to_apply=%region_2.3 | all-reduce | flops 3120 | bytes 18816 | tf_op jit(solution)/shard_map/psum | solution.py:77
  255.2 1.8 convolution_bitcast_fusion
  257.0 0.0 reduce-scatter.2.cloned.1.call-update
  257.1 64.0 %all-reduce.4.cloned.1.call-done = f32[48,8192]{1,0:T(8,128)} async-done(((f32[48,8192]{1,0:T(8,128)}), f32[48,8192]{1,0:T(8,128)}) %all-reduce.4.cloned.1.call-update) | async-done | bytes 1572880 | tf_op jit(solution)/shard_map/psum | solution.py:77
  321.1 0.0 copy-done.1
  321.1 1.8 fusion
  322.8 0.0 copy-start.3
  322.9 0.9 copy.51
  323.8 9.3 %all-to-all-start = ((bf16[48,32,256]{2,0,1:T(8,128)(2,1)}), bf16[48,32,256]{2,0,1:T(8,128)(2,1)S(1)}, u32[]{:S(2)}, u32[]{:S(2)}) async-start(bf16[48,32,256]{2,0,1:T(8,128)(2,1)} %bitcast.28), calls=%async_computation | async-start | bytes 1572864 | tf_op jit(solution)/shard_map/all_to_all | solution.py:84
  333.1 0.0 copy-done.3
  333.1 1.2 scatter_custom_fusion
  334.3 0.0 copy-start.2
  334.3 23.0 %all-to-all-done = bf16[48,32,256]{2,0,1:T(8,128)(2,1)S(1)} async-done(((bf16[48,32,256]{2,0,1:T(8,128)(2,1)}), bf16[48,32,256]{2,0,1:T(8,128)(2,1)S(1)}, u32[]{:S(2)}, u32[]{:S(2)}) %all-to-all-start) | async-done | bytes 786464 | tf_op jit(solution)/shard_map/all_to_all | solution.py:84
  357.3 123.7 %all-reduce.6.cloned.1.call-done = f32[64,512]{1,0:T(8,128)} async-done(((f32[64,512]{1,0:T(8,128)}), f32[64,512]{1,0:T(8,128)}) %all-reduce.6.cloned.1.call-update) | async-done | bytes 131088 | tf_op jit(solution)/shard_map/psum | solution.py:96
  481.0 224.9 %reduce-scatter.2.cloned.1.call-done = f32[256,64]{0,1:T(8,128)} async-done(((f32[8192,64]{0,1:T(8,128)}), f32[256,64]{0,1:T(8,128)}) %reduce-scatter.2.cloned.1.call-update) | async-done | bytes 65552 | tf_op jit(solution)/shard_map/reduce_scatter | solution.py:87
  705.9 0.9 copy.59
  706.7 1.6 copy.60
  708.3 0.0 copy-done.2
  (4 shorter events, 0.0 us)
Async XLA Ops:
  7.2 196.3 %copy-start = (bf16[48,8192]{1,0:T(8,128)(2,1)S(1)}, bf16[48,8192]{1,0:T(8,128)(2,1)}, u32[]{:S(2)}) copy-start(bf16[48,8192]{1,0:T(8,128)(2,1)} %param.11) | copy-start | bytes 2359300
  7.2 5.1 copy-start.7
  7.2 5.1 copy-start.4
  7.2 118.8 %copy-start.6 = (f32[48]{0:T(128)S(1)}, f32[48]{0:T(128)}, u32[]{:S(2)}) copy-start(f32[48]{0:T(128)} %param.16) | copy-start | bytes 580
  7.2 118.8 %all-gather.3.cloned.1.call-start = ((), (), s32[]{:S(2)}) async-start(), calls=%async_computation.2 | async-start | bytes 8650752 | tf_op jit(solution)/shard_map/all_gather | solution.py:60
  10.8 192.6 %all-gather.5.cloned.1.call-start = ((), (), s32[]{:S(2)}) async-start(), calls=%async_computation.3 | async-start | bytes 1081344 | tf_op jit(solution)/shard_map/all_gather | solution.py:61
  11.5 309.5 %all-reduce.4.cloned.1.call-start = ((), (), s32[]{:S(2)}) async-start(), calls=%async_computation.4 | async-start | bytes 3145728 | tf_op jit(solution)/shard_map/psum | solution.py:77
  13.0 119.2 %copy-start.5 = (bf16[64,512]{1,0:T(8,128)(2,1)S(1)}, bf16[64,512]{1,0:T(8,128)(2,1)}, u32[]{:S(2)}) copy-start(bf16[64,512]{1,0:T(8,128)(2,1)} %param.15) | copy-start | bytes 196612
  132.1 348.8 %all-reduce.6.cloned.1.call-start = ((), (), s32[]{:S(2)}) async-start(), calls=%async_computation.6 | async-start | bytes 262144 | tf_op jit(solution)/shard_map/psum | solution.py:96
  206.0 499.8 %reduce-scatter.2.cloned.1.call-start = ((), (), s32[]{:S(2)}) async-start(), calls=%async_computation.5 | async-start | bytes 2162688 | tf_op jit(solution)/shard_map/reduce_scatter | solution.py:87
  255.2 65.8 %copy-start.1 = (bf16[8192,64]{0,1:T(8,128)(2,1)S(1)}, bf16[8192,64]{0,1:T(8,128)(2,1)}, u32[]{:S(2)}) copy-start(bf16[8192,64]{0,1:T(8,128)(2,1)} %all-gather.5.cloned.1.call-done) | copy-start | bytes 3145732
  322.8 10.2 %copy-start.3 = (bf16[192,512]{1,0:T(8,128)(2,1)S(1)}, bf16[192,512]{1,0:T(8,128)(2,1)}, u32[]{:S(2)}) copy-start(bf16[192,512]{1,0:T(8,128)(2,1)} %param.10) | copy-start | bytes 589828
  323.8 33.5 %all-to-all-start = ((bf16[48,32,256]{2,0,1:T(8,128)(2,1)}), bf16[48,32,256]{2,0,1:T(8,128)(2,1)S(1)}, u32[]{:S(2)}, u32[]{:S(2)}) async-start(bf16[48,32,256]{2,0,1:T(8,128)(2,1)} %bitcast.28), calls=%async_computation | async-start | bytes 1572864 | tf_op jit(solution)/shard_map/all_to_all | solution.py:84
  334.3 374.0 %copy-start.2 = (bf16[192,512]{1,0:T(8,128)(2,1)}, bf16[192,512]{1,0:T(8,128)(2,1)S(1)}, u32[]{:S(2)}) copy-start(bf16[192,512]{1,0:T(8,128)(2,1)S(1)} %scatter_custom_fusion) | copy-start | bytes 589828
Sparse Core Ops, SparseCore 0:
  11.7 114.2 all-gather.2
  129.0 74.3 all-gather.4
  205.8 115.2 all-reduce.3
  325.3 155.5 all-reduce.5
  485.8 220.0 reduce-scatter.1
where the time goes:
time: 715 us
  waiting for transfers between devices  620 us (87%)
  blocking collectives  42.8 us (6%)
  matrix products  18.8 us (3%)
  between operations  14.6 us (2%)
  starting transfers between devices  9.47 us (1%)
    reduce_scatter x1, waiting for transfers between devices, body(): lax.psum_scatter(jnp.dot(attention.T, adapter_rank_gradient, preferred_el...  225 us
    psum x1, waiting for transfers between devices, body(): adapter_up_gradient = lax.psum(up_factor_piece, 'seq')  124 us
    all_gather x1, waiting for transfers between devices, body(): lax.all_gather(projection_weight, 'seq', axis=0, tiled=True)  113 us
    all_gather x1, waiting for transfers between devices, body(): lax.all_gather(adapter_down, 'seq', axis=0, tiled=True)  71 us
    psum x1, waiting for transfers between devices, body(): lax.psum((head_part, adapter_rank_piece, gate_part), 'tp')  64 us
    psum x1, blocking collectives, body(): lax.psum((head_part, adapter_rank_piece, gate_part), 'tp')  42.8 us
    all_to_all x1, waiting for transfers between devices, body(): lax.all_to_all(home_grad, 'seq', split_axis=1, concat_axis=0, tiled=True)  23 us
  transfers between devices with their start and end apart: 6, of which 6 were waited for; matrix products, arithmetic and copies ran while one was open for 3% of the time, Pallas kernels for 0%

commit v1 on v0

--- a/solution.py
+++ b/solution.py
@@ -2,6 +2,7 @@
 import jax.numpy as jnp
 from jax import lax
 from jax.sharding import PartitionSpec as P
+from jax.lax import all_to_all, axis_size
 
 LEVELS = (
     -1.0,
@@ -22,6 +23,12 @@
     1.0,
 )
 adapter_scale = 0.25
+
+
+def follow_signs_up(xx):
+    return jnp.concatenate(
+        all_to_all(jnp.stack([xx for _ in range(axis_size("seq"))]), "seq", 0, 0), axis=0
+    )
 
 
 def precise_matmul(left, right):
@@ -57,7 +64,7 @@
     live_slot = jnp.arange(home_slots, dtype=jnp.int32) < counts[0]
     target = jnp.where(live_slot, selected, residual.shape[0])
     full_w, full_a = (
-        lax.all_gather(projection_weight, "seq", axis=0, tiled=True),
+        follow_signs_up(projection_weight),
         lax.all_gather(adapter_down, "seq", axis=0, tiled=True),
     )
     adapter_product = jnp.dot(attention, full_a, preferred_element_type=jnp.float32)

time: 715 us -> 745 us (1.042)
  starting transfers between devices: 9.47 us -> 22.8 us
  waiting for transfers between devices: 620 us -> 629 us
    all_to_all x0 -> x1, waiting for transfers between devices: none -> 192 us  [follow_signs_up(): all_to_all(jnp.stack([xx for _ in range(axis_size('seq'))]), 'seq', 0, 0)]
    all_gather x1 -> x0, waiting for transfers between devices: 113 us -> none  [body(): lax.all_gather(projection_weight, 'seq', axis=0, tiled=True)]
    all_gather x1, waiting for transfers between devices: 71 us -> 0.02 us  [body(): lax.all_gather(adapter_down, 'seq', axis=0, tiled=True)]
    all_to_all x0 -> x1, starting transfers between devices: none -> 13.4 us  [follow_signs_up(): all_to_all(jnp.stack([xx for _ in range(axis_size('seq'))]), 'seq', 0, 0)]
  transfers between devices with their start and end apart: 6 -> 6, of which waited for: 6 -> 5; matrix products, arithmetic and copies ran while one was open for 3% -> 3% of each run, Pallas kernels for 0% -> 0%
where the time goes in v1:
time: 745 us
  waiting for transfers between devices  629 us (84%)
  blocking collectives  45.4 us (6%)
  starting transfers between devices  22.8 us (3%)
  matrix products  18.7 us (3%)
  between operations  16.5 us (2%)
  local copies, waits for them, and re-layouts  9.73 us (1%)
    reduce_scatter x1, waiting for transfers between devices, body(): lax.psum_scatter(jnp.dot(attention.T, adapter_rank_gradient, preferred_el...  225 us
    all_to_all x1, waiting for transfers between devices, follow_signs_up(): all_to_all(jnp.stack([xx for _ in range(axis_size('seq'))]), 'seq', 0, 0)  192 us
    psum x1, waiting for transfers between devices, body(): adapter_up_gradient = lax.psum(up_factor_piece, 'seq')  123 us
    psum x1, waiting for transfers between devices, body(): lax.psum((head_part, adapter_rank_piece, gate_part), 'tp')  64.8 us
    psum x1, blocking collectives, body(): lax.psum((head_part, adapter_rank_piece, gate_part), 'tp')  45.4 us
    all_to_all x1, waiting for transfers between devices, body(): lax.all_to_all(home_grad, 'seq', split_axis=1, concat_axis=0, tiled=True)  23.1 us
  transfers between devices with their start and end apart: 6, of which 5 were waited for; matrix products, arithmetic and copies ran while one was open for 3% of the time, Pallas kernels for 0%

profile of v1, /device:TPU:8, one launch (start us, length us, event | category | flops | bytes accessed | tf_op | source)
XLA Modules:
  0.0 744.6 jit_solution(6507905423675193379)
XLA Ops:
  8.0 0.0 copy-start
  8.0 1.3 copy.34
  9.3 1.5 fusion.2
  10.8 0.1 copy.49
  11.0 4.2 stack.2
  15.1 0.0 copy-start.7
  15.1 13.4 %all-to-all-start = ((bf16[32,256,512]{2,1,0:T(8,128)(2,1)}), bf16[32,256,512]{2,1,0:T(8,128)(2,1)}, u32[]{:S(2)}, u32[]{:S(2)}) async-start(bf16[32,256,512]{2,1,0:T(8,128)(2,1)} %stack.2), calls=%async_computation | async-start | bytes 16777216 | tf_op jit(solution)/shard_map/all_to_all | solution.py:30
  28.6 0.0 copy-start.5
  28.6 0.0 all-gather.2.cloned.1.call-start
  28.6 0.7 all-gather.2.cloned.1.call-update
  29.3 0.0 all-reduce.4.cloned.1.call-start
  30.0 0.0 copy-done.7
  30.1 0.0 copy-done.4
  30.1 0.7 gather_fusion
  30.8 191.6 %all-to-all-done = bf16[32,256,512]{2,1,0:T(8,128)(2,1)} async-done(((bf16[32,256,512]{2,1,0:T(8,128)(2,1)}), bf16[32,256,512]{2,1,0:T(8,128)(2,1)}, u32[]{:S(2)}, u32[]{:S(2)}) %all-to-all-start) | async-done | bytes 8388640 | tf_op jit(solution)/shard_map/all_to_all | solution.py:30
  222.3 0.0 copy-done.6
  222.3 7.1 fusion.8
  229.4 0.0 all-reduce.4.cloned.1.call-update
  229.4 0.0 all-reduce.6.cloned.1.call-start
  229.5 0.0 copy-done.5
  229.5 0.2 convolution_multiply_fusion.2
  229.7 0.0 all-gather.2.cloned.1.call-done
  229.7 0.0 copy-done
  229.7 1.6 fusion.9
  231.4 0.2 convolution_multiply_fusion.1
  231.5 0.9 convolution_multiply_fusion
  232.5 0.0 all-reduce.6.cloned.1.call-update
  232.5 0.0 copy-start.1
  232.5 0.0 reduce-scatter.2.cloned.1.call-start
  232.6 5.1 multiply_reduce_fusion
  237.7 0.0 copy-start.3
  237.7 45.4 %all-reduce = (bf16[48,64]{1,0:T(8,128)(2,1)S(1)}, f32[48]{0:T(128)}) all-reduce(f32[48,64]{1,0:T(8,128)S(1)} %convolution_multiply_fusion.2, f32[48]{0:T(128)S(1)} %get-tuple-element.9), channel_id=1, replica_groups=mesh['seq'=32,'tp'=16] {'tp'}, use_global_device_ids=true, to_apply=%region_2.3 | all-reduce | flops 3120 | bytes 18816 | tf_op jit(solution)/shard_map/psum | solution.py:84
  283.1 1.8 convolution_bitcast_fusion
  284.9 0.0 reduce-scatter.2.cloned.1.call-update
  284.9 64.8 %all-reduce.4.cloned.1.call-done = f32[48,8192]{1,0:T(8,128)} async-done(((f32[48,8192]{1,0:T(8,128)}), f32[48,8192]{1,0:T(8,128)}) %all-reduce.4.cloned.1.call-update) | async-done | bytes 1572880 | tf_op jit(solution)/shard_map/psum | solution.py:84
  349.7 0.0 copy-done.1
  349.7 1.8 fusion
  351.5 0.9 copy.53
  352.4 9.2 %all-to-all-start.1 = ((bf16[48,32,256]{2,0,1:T(8,128)(2,1)}), bf16[48,32,256]{2,0,1:T(8,128)(2,1)S(1)}, u32[]{:S(2)}, u32[]{:S(2)}) async-start(bf16[48,32,256]{2,0,1:T(8,128)(2,1)} %bitcast.31), calls=%async_computation.1 | async-start | bytes 1572864 | tf_op jit(solution)/shard_map/all_to_all | solution.py:91
  361.7 0.0 copy-done.3
  361.7 1.2 scatter_custom_fusion
  362.9 0.0 copy-start.2
  362.9 23.1 %all-to-all-done.1 = bf16[48,32,256]{2,0,1:T(8,128)(2,1)S(1)} async-done(((bf16[48,32,256]{2,0,1:T(8,128)(2,1)}), bf16[48,32,256]{2,0,1:T(8,128)(2,1)S(1)}, u32[]{:S(2)}, u32[]{:S(2)}) %all-to-all-start.1) | async-done | bytes 786464 | tf_op jit(solution)/shard_map/all_to_all | solution.py:91
  386.0 123.4 %all-reduce.6.cloned.1.call-done = f32[64,512]{1,0:T(8,128)} async-done(((f32[64,512]{1,0:T(8,128)}), f32[64,512]{1,0:T(8,128)}) %all-reduce.6.cloned.1.call-update) | async-done | bytes 131088 | tf_op jit(solution)/shard_map/psum | solution.py:103
  509.4 225.2 %reduce-scatter.2.cloned.1.call-done = f32[256,64]{0,1:T(8,128)} async-done(((f32[8192,64]{0,1:T(8,128)}), f32[256,64]{0,1:T(8,128)}) %reduce-scatter.2.cloned.1.call-update) | async-done | bytes 65552 | tf_op jit(solution)/shard_map/reduce_scatter | solution.py:94
  734.5 0.9 copy.61
  735.4 1.6 copy.62
  737.0 0.0 copy-done.2
  (5 shorter events, 0.0 us)
Async XLA Ops:
  8.0 221.7 %copy-start = (bf16[48,8192]{1,0:T(8,128)(2,1)S(1)}, bf16[48,8192]{1,0:T(8,128)(2,1)}, u32[]{:S(2)}) copy-start(bf16[48,8192]{1,0:T(8,128)(2,1)} %param.11) | copy-start | bytes 2359300
  15.1 14.9 %copy-start.7 = (s32[48]{0:T(128)S(1)}, s32[48]{0:T(128)}, u32[]{:S(2)}) copy-start(s32[48]{0:T(128)} %param.17) | copy-start | bytes 580
  15.1 14.9 %copy-start.4 = (bf16[192,512]{1,0:T(8,128)(2,1)S(1)}, bf16[192,512]{1,0:T(8,128)(2,1)}, u32[]{:S(2)}) copy-start(bf16[192,512]{1,0:T(8,128)(2,1)} %param.19) | copy-start | bytes 589828
  15.1 207.2 %copy-start.6 = (f32[48]{0:T(128)S(1)}, f32[48]{0:T(128)}, u32[]{:S(2)}) copy-start(f32[48]{0:T(128)} %param.16) | copy-start | bytes 580
  15.1 207.2 %all-to-all-start = ((bf16[32,256,512]{2,1,0:T(8,128)(2,1)}), bf16[32,256,512]{2,1,0:T(8,128)(2,1)}, u32[]{:S(2)}, u32[]{:S(2)}) async-start(bf16[32,256,512]{2,1,0:T(8,128)(2,1)} %stack.2), calls=%async_computation | async-start | bytes 16777216 | tf_op jit(solution)/shard_map/all_to_all | solution.py:30
  28.6 200.9 %copy-start.5 = (bf16[64,512]{1,0:T(8,128)(2,1)S(1)}, bf16[64,512]{1,0:T(8,128)(2,1)}, u32[]{:S(2)}) copy-start(bf16[64,512]{1,0:T(8,128)(2,1)} %param.15) | copy-start | bytes 196612
  28.6 201.1 %all-gather.2.cloned.1.call-start = ((), (), s32[]{:S(2)}) async-start(), calls=%async_computation.3 | async-start | bytes 1081344 | tf_op jit(solution)/shard_map/all_gather | solution.py:68
  29.3 320.4 %all-reduce.4.cloned.1.call-start = ((), (), s32[]{:S(2)}) async-start(), calls=%async_computation.4 | async-start | bytes 3145728 | tf_op jit(solution)/shard_map/psum | solution.py:84
  229.4 279.9 %all-reduce.6.cloned.1.call-start = ((), (), s32[]{:S(2)}) async-start(), calls=%async_computation.6 | async-start | bytes 262144 | tf_op jit(solution)/shard_map/psum | solution.py:103
  232.5 117.2 %copy-start.1 = (bf16[8192,64]{0,1:T(8,128)(2,1)S(1)}, bf16[8192,64]{0,1:T(8,128)(2,1)}, u32[]{:S(2)}) copy-start(bf16[8192,64]{0,1:T(8,128)(2,1)} %all-gather.2.cloned.1.call-done) | copy-start | bytes 3145732
  232.5 502.0 %reduce-scatter.2.cloned.1.call-start = ((), (), s32[]{:S(2)}) async-start(), calls=%async_computation.5 | async-start | bytes 2162688 | tf_op jit(solution)/shard_map/reduce_scatter | solution.py:94
  237.7 124.0 %copy-start.3 = (bf16[192,512]{1,0:T(8,128)(2,1)S(1)}, bf16[192,512]{1,0:T(8,128)(2,1)}, u32[]{:S(2)}) copy-start(bf16[192,512]{1,0:T(8,128)(2,1)} %param.10) | copy-start | bytes 589828
  352.4 33.6 %all-to-all-start.1 = ((bf16[48,32,256]{2,0,1:T(8,128)(2,1)}), bf16[48,32,256]{2,0,1:T(8,128)(2,1)S(1)}, u32[]{:S(2)}, u32[]{:S(2)}) async-start(bf16[48,32,256]{2,0,1:T(8,128)(2,1)} %bitcast.31), calls=%async_computation.1 | async-start | bytes 1572864 | tf_op jit(solution)/shard_map/all_to_all | solution.py:91
  362.9 374.1 %copy-start.2 = (bf16[192,512]{1,0:T(8,128)(2,1)}, bf16[192,512]{1,0:T(8,128)(2,1)S(1)}, u32[]{:S(2)}) copy-start(bf16[192,512]{1,0:T(8,128)(2,1)S(1)} %scatter_custom_fusion) | copy-start | bytes 589828
Sparse Core Ops, SparseCore 0:
  32.5 124.6 all-gather.1
Sparse Core Ops, SparseCore 1:
  229.5 120.1 all-reduce.3
  354.0 155.3 all-reduce.5
  514.2 220.3 reduce-scatter.1
